TPU v7x, 512 devices: a whole 4x4x16 slice. The times are simulated.
512 devices in a mesh: dp: 64 (over x, z), mp: 8 (over y, core).
Axes of the slice: x: 4, y: 4, z: 16, core: 2. Of those that a mesh axis runs over, the one named last changes fastest.
Arguments:
- layer_input: float32 [16384, 512], P('dp'), may hold values from -6 to 6
- grad_out: float32 [16384, 512], P('dp'), may hold values from -6 to 6
- segment: int32 [64, 256], P('dp'), may hold values from 0 to 7, never falling along the last dimension, each value on 1 to 128 neighbouring positions
- item_ids: int32 [16384], P('dp'), may hold values from 0 to 511
- w_uvqk: float32 [512, 2048], P(None, 'mp'), may hold values from -0.25 to 0.25
- w_out: float32 [512, 512], P('mp'), may hold values from -0.25 to 0.25
- table: float32 [512, 512], P(('dp', 'mp')), may hold values from -6 to 6
- accum: float32 [512], P(('dp', 'mp')), may hold values from 0.1 to 2
Outputs:
- w_uvqk_grad: float32 [512, 2048], P(None, 'mp')
- w_out_grad: float32 [512, 512], P('mp')
- new_table: float32 [512, 512], P(('dp', 'mp'))
- new_accum: float32 [512], P(('dp', 'mp'))
Inputs may be any that keep to these rules, and one draw needn't show every extreme that they name: `segment`: segment numbers never fall along a row; a history holds at most 128 tokens and some history holds exactly that many.
All inputs are finite; a program needn't handle non-finite values.
Results may differ from a plain program's by a relative error of at most 0.0003.
Values sent between devices are 32-bit elements; how exact they have to be, the bound alone decides.
No kernel may reach another device: no remote copies, remote signals or barrier semaphores. Data moves between devices by JAX's collectives and lax.ppermute only.
A program may use at most 64 MiB of HBM per device.

v0:
```python
import jax
import jax.numpy as jnp
from jax import lax
from jax.sharding import PartitionSpec as P

HEAD_DIM = 64


highest = lax.Precision.HIGHEST


def mdot(left, right):
    return jnp.dot(left, right, precision=highest, preferred_element_type=jnp.float32)


def onehot_sum(item_ids, targets, values):
    table_hits = (item_ids[:, None] == targets[None, :]).astype(jnp.float32)
    return lax.dot_general(
        table_hits,
        values,
        (((0,), (0,)), ((), ())),
        precision=highest,
        preferred_element_type=jnp.float32,
    )


def body(layer_input, grad_out, segment, item_ids, w_uvqk, w_out, table, accum):
    count = layer_input.shape[0]
    width = layer_input.shape[1]
    local = w_uvqk.shape[1] // (4 * HEAD_DIM)
    scale = HEAD_DIM ** (-0.5)
    pre = mdot(layer_input, w_uvqk).reshape(count, local, 4, HEAD_DIM)
    act = jax.nn.silu(pre)
    ublk, vblk, qblk, kblk = (act[:, :, 0], act[:, :, 1], act[:, :, 2], act[:, :, 3])
    seg_row = segment[0]
    place = jnp.arange(count)
    mask = ((seg_row[:, None] == seg_row[None, :]) & (place[:, None] >= place[None, :])).astype(
        jnp.float32
    )
    score = jnp.einsum("ihd,jhd->hij", qblk, kblk, precision=highest) * scale
    sigm = jax.nn.sigmoid(score)
    attn = score * sigm * mask
    outv = jnp.einsum("hij,jhd->ihd", attn, vblk, precision=highest).reshape(
        count, local * HEAD_DIM
    )
    sums = lax.psum((jnp.sum(outv, axis=1), jnp.sum(outv * outv, axis=1)), "mp")
    mean = sums[0][:, None] / width
    var = sums[1][:, None] / width - mean * mean
    rstd = lax.rsqrt(var + 1e-05)
    normed = (outv - mean) * rstd
    nheads = normed.reshape(count, local, HEAD_DIM)
    zval = (nheads * ublk).reshape(count, local * HEAD_DIM)
    dzval = mdot(grad_out, w_out.T).reshape(count, local, HEAD_DIM)
    w_out_part = mdot(zval.T, grad_out)
    dnorm = (dzval * ublk).reshape(count, local * HEAD_DIM)
    dublk = dzval * nheads
    grads_sum = lax.psum((jnp.sum(dnorm, axis=1), jnp.sum(dnorm * normed, axis=1)), "mp")
    first = grads_sum[0][:, None] / width
    second = grads_sum[1][:, None] / width
    dout = (rstd * (dnorm - first - normed * second)).reshape(count, local, HEAD_DIM)
    dattn = jnp.einsum("ihd,jhd->hij", dout, vblk, precision=highest)
    dvblk = jnp.einsum("hij,ihd->jhd", attn, dout, precision=highest)
    dscore = dattn * mask * (sigm * (1.0 + score * (1.0 - sigm))) * scale
    dqblk = jnp.einsum("hij,jhd->ihd", dscore, kblk, precision=highest)
    dkblk = jnp.einsum("hij,ihd->jhd", dscore, qblk, precision=highest)
    dact = jnp.stack([dublk, dvblk, dqblk, dkblk], axis=2)
    psig = jax.nn.sigmoid(pre)
    dpre = (dact * psig * (1.0 + pre * (1.0 - psig))).reshape(count, local * 4 * HEAD_DIM)
    w_uvqk_part = mdot(layer_input.T, dpre)
    w_uvqk_grad, w_out_grad = lax.psum((w_uvqk_part, w_out_part), "dp")
    head_part = mdot(dpre, w_uvqk.T)
    own_rows = table.shape[0]
    n_dp = lax.axis_size("dp")
    n_mp = lax.axis_size("mp")
    first_head = (lax.axis_index("mp") == 0).astype(jnp.float32)
    term = head_part + grad_out * first_head
    targets = jnp.arange(own_rows * n_dp * n_mp, dtype=jnp.int32)
    slab = onehot_sum(item_ids, targets, term)
    row_grad = lax.psum_scatter(slab, ("dp", "mp"), scatter_dimension=0, tiled=True)
    new_accum = accum + jnp.sum(row_grad * row_grad, axis=1) / width
    new_table = table - 0.5 * row_grad * lax.rsqrt(new_accum)[:, None]
    return (w_uvqk_grad, w_out_grad, new_table, new_accum)


def solution(mesh):
    placed = (
        P("dp", None),
        P("dp", None),
        P("dp", None),
        P("dp"),
        P(None, "mp"),
        P("mp", None),
        P(("dp", "mp"), None),
        P(("dp", "mp")),
    )
    return jax.shard_map(
        body,
        mesh=mesh,
        in_specs=placed,
        out_specs=(P(None, "mp"), P("mp", None), P(("dp", "mp"), None), P(("dp", "mp"))),
        check_vma=False,
    )
```

profile of v0, /device:TPU:1, one launch (start us, length us, event | category | flops | bytes accessed | tf_op | source)
XLA Modules:
  0.0 792.0 jit_solution(18049761097423142896)
XLA Ops:
  7.2 1.0 copy-done
  8.2 2.0 fusion.22
  10.3 0.4 convolution_multiply_fusion
  10.8 0.7 copy-done.7
  11.5 0.4 fusion.12
  11.9 18.6 %all-reduce.3 = (f32[256]{0:T(256)S(1)}, f32[256]{0:T(256)S(1)}) all-reduce(f32[256]{0:T(256)S(1)} %get-tuple-element.24, f32[256]{0:T(256)S(1)} %reduce_sum.45), channel_id=1, replica_groups=mesh['dp'=64,'mp'=8] {'mp'}, use_global_device_ids=true, to_apply=%region_3.4 | all-reduce | flops 512 | bytes 4096 | tf_op jit(solution)/shard_map/psum | solution.py:46
  30.5 0.6 fusion.21
  31.1 12.4 %all-reduce.2 = (f32[256]{0:T(256)S(1)}, f32[256]{0:T(256)S(1)}) all-reduce(f32[256]{0:T(256)S(1)} %get-tuple-element.13, f32[256]{0:T(256)S(1)} %get-tuple-element.12), channel_id=1, replica_groups=mesh['dp'=64,'mp'=8] {'mp'}, use_global_device_ids=true, to_apply=%region_7.8 | all-reduce | flops 512 | bytes 4096 | tf_op jit(solution)/shard_map/psum | solution.py:57
  43.6 0.5 convolution_bitcast_fusion.3
  44.0 0.5 fusion.1
  44.5 0.2 convolution_bitcast_fusion.2
  44.7 0.4 convolution_bitcast_fusion.1
  45.1 0.1 fusion.3
  45.3 1.1 convolution_add_fusion
  46.3 1.7 fusion.2
  48.2 1.1 fusion.6
  49.3 1.4 convolution_bitcast_fusion
  51.4 469.3 %all-reduce.7.cloned.1.call-done = f32[512,512]{1,0:T(8,128)} async-done(((f32[512,512]{1,0:T(8,128)}), f32[512,512]{1,0:T(8,128)}) %all-reduce.7.cloned.1.call-update) | async-done | bytes 1048592
  520.7 1.3 multiply_reduce_fusion.1
  522.8 0.7 copy-done.5
  523.4 1.3 multiply_subtract_fusion
  524.7 256.6 %all-reduce.9.cloned.1.call-done = (f32[512,256]{0,1:T(8,128)}, f32[64,512]{1,0:T(8,128)}) async-done(((f32[512,256]{0,1:T(8,128)}, f32[64,512]{1,0:T(8,128)}), (f32[512,256]{0,1:T(8,128)}, f32[64,512]{1,0:T(8,128)})) %all-reduce.9.cloned.1.call-update) | async-done | bytes 655376 | tf_op jit(solution)/shard_map/psum | solution.py:70
  781.3 2.1 copy.17
  783.4 0.7 copy.24
  (22 shorter events, 0.3 us)
Async XLA Ops:
  7.2 1.0 copy-start
  7.2 513.5 %all-reduce.7.cloned.1.call-start = ((), (), s32[]{:S(2)}) async-start(), calls=%async_computation | async-start | bytes 2097152
  10.8 0.7 copy-start.7
  11.4 19.0 %copy-start.1 = (f32[256,512]{1,0:T(8,128)S(1)}, f32[256,512]{1,0:T(8,128)}, u32[]{:S(2)}) copy-start(f32[256,512]{1,0:T(8,128)} %param.9) | copy-start | bytes 1572868
  11.5 19.0 %copy-start.3 = (f32[64,512]{1,0:T(8,128)S(1)}, f32[64,512]{1,0:T(8,128)}, u32[]{:S(2)}) copy-start(f32[64,512]{1,0:T(8,128)} %param.13) | copy-start | bytes 393220
  45.2 1.1 copy-start.6
  48.1 1.2 copy-start.2
  48.1 733.2 %all-reduce.9.cloned.1.call-start = ((), (), s32[]{:S(2)}) async-start(), calls=%async_computation.1 | async-start | bytes 1310720 | tf_op jit(solution)/shard_map/psum | solution.py:70
  522.7 0.7 copy-start.5
  781.3 2.1 copy-start.4
Sparse Core Ops, SparseCore 0:
  48.2 472.4 all-reduce.6
  524.7 256.5 all-reduce.8
where the time goes:
time: 802 us; the launch traced here: 792 us
  waiting for transfers between devices  726 us (91%)
  blocking collectives  31 us (4%)
  between operations  16.6 us (2%)
  matrix products  10.3 us (1%)
    unnamed x3, waiting for transfers between devices  469 us
    psum x1, waiting for transfers between devices, body(): w_uvqk_grad, w_out_grad = lax.psum((w_uvqk_part, w_out_part), 'dp')  257 us
    psum x1, blocking collectives, body(): sums = lax.psum((jnp.sum(outv, axis=1), jnp.sum(outv * outv, axis=1)), 'mp')  18.6 us
  transfers between devices with their start and end apart: 2, of which 2 were waited for; matrix products, arithmetic and copies ran while one was open for 1% of the time, Pallas kernels for 0%

commit v1 on v0

v1 whole, which is shorter than its diff:
```python
import jax
import jax.numpy as jnp
from jax import lax
from jax.sharding import Mesh
from jax.sharding import PartitionSpec as P

HEAD_DIM = 64
HIGH = lax.Precision.HIGH
MP = ("y", "c")
DP = ("x", "z")


def dot(left, right, dims):
    return lax.dot_general(
        left, right, ((dims[:1], dims[1:]), ((), ())),
        precision=HIGH, preferred_element_type=jnp.float32,
    )


def body(layer_input, grad_out, segment, item_ids, w_uvqk, w_out, table, accum):
    count, width = layer_input.shape
    hd = HEAD_DIM
    scale = hd ** (-0.5)
    n_x, n_z = lax.axis_size("x"), lax.axis_size("z")
    n_mp = lax.axis_size(MP)
    pre = dot(layer_input, w_uvqk, (1, 0))
    psig = jax.nn.sigmoid(pre)
    act = pre * psig
    ublk, vblk, qblk, kblk = (act[:, i * hd:(i + 1) * hd] for i in range(4))
    seg_row = segment[0]
    place = jnp.arange(count)
    mask = ((seg_row[:, None] == seg_row[None, :]) & (place[:, None] >= place[None, :])).astype(jnp.float32)
    score = dot(qblk, kblk, (1, 1)) * scale
    sigm = jax.nn.sigmoid(score)
    attn = score * sigm * mask
    outv = dot(attn, vblk, (1, 0))
    dzval = dot(grad_out, w_out, (1, 1))
    dnorm = dzval * ublk
    stats = jnp.stack([
        jnp.sum(outv, axis=1), jnp.sum(outv * outv, axis=1),
        jnp.sum(dnorm, axis=1), jnp.sum(dnorm * outv, axis=1),
    ]).reshape(8, count // 2)
    stats = jnp.broadcast_to(stats[None], (n_mp,) + stats.shape)
    stats = jnp.sum(lax.all_to_all(stats, MP, 0, 0, tiled=True), axis=0).reshape(4, count)
    mean = stats[0] / width
    var = stats[1] / width - mean * mean
    rstd = lax.rsqrt(var + 1e-05)
    first = stats[2] / width
    second = rstd * (stats[3] - mean * stats[2]) / width
    mean, rstd, first, second = (t[:, None] for t in (mean, rstd, first, second))
    normed = (outv - mean) * rstd
    zval = normed * ublk
    dublk = dzval * normed
    dout = rstd * (dnorm - first - normed * second)
    dattn = dot(dout, vblk, (1, 1))
    dvblk = dot(attn, dout, (0, 0))
    dscore = dattn * mask * (sigm * (1.0 + score * (1.0 - sigm))) * scale
    dqblk = dot(dscore, kblk, (1, 0))
    dkblk = dot(dscore, qblk, (0, 0))
    dact = jnp.concatenate([dublk, dvblk, dqblk, dkblk], axis=1)
    dpre = dact * psig * (1.0 + pre * (1.0 - psig))
    head_part = dot(w_uvqk, dpre, (1, 1)).reshape(n_mp, width // n_mp, count)
    head_part = lax.all_to_all(head_part, MP, 0, 0, tiled=True)
    fblk = width // n_mp
    own = lax.dynamic_slice(grad_out, (0, lax.axis_index(MP) * fblk), (count, fblk))
    xgrad = jnp.sum(head_part, axis=0).T + own
    rows = n_x * n_z * n_mp
    half = n_mp // 2
    ids = jnp.arange(rows // 2, dtype=jnp.int32)
    target = (ids // half) * n_mp + ids % half
    slab = jnp.concatenate([
        dot((t[:, None] == item_ids[None, :]).astype(jnp.float32), xgrad, (1, 0))
        for t in (target, target + half)
    ], axis=1).reshape(n_x, n_z, half, 2 * fblk)
    w1 = dot(layer_input, dpre, (0, 0))
    w2 = dot(zval, grad_out, (0, 0))
    w1c = w1.reshape(n_x, n_z, 8, 2, 128).transpose(0, 1, 3, 2, 4).reshape(n_x, n_z, 16, 128)
    w2c = w2.reshape(n_z, 4, n_x, 128).transpose(2, 0, 1, 3)
    buf = jnp.concatenate([w1c, w2c, slab], axis=2).reshape(n_x, n_z * 24, 128)
    buf = jnp.sum(lax.all_to_all(buf, "x", 0, 0, tiled=True), axis=0).reshape(n_z, 24, 128)
    buf = jnp.sum(lax.all_to_all(buf, "z", 0, 0, tiled=True), axis=0)
    mine = buf[20:].reshape(half, 2, fblk).transpose(1, 0, 2).reshape(n_mp, fblk)
    row_grad = lax.all_to_all(mine, MP, 0, 0, tiled=True).reshape(1, width)
    new_accum = accum + jnp.sum(row_grad * row_grad, axis=1) / width
    new_table = table - 0.5 * row_grad * lax.rsqrt(new_accum)[:, None]
    full = jnp.broadcast_to(buf[None], (n_z, 24, 128))
    full = lax.all_to_all(full, "z", 0, 0, tiled=True)
    full = lax.all_gather(full, "x", tiled=False)
    w1g = full[:, :, :16].reshape(n_x, n_z, 2, 8, 128).transpose(0, 1, 3, 2, 4).reshape(width, 4 * hd)
    w2g = full[:, :, 16:20].transpose(1, 2, 0, 3).reshape(hd, width)
    return (w1g, w2g, new_table, new_accum)


def solution(mesh):
    split = Mesh(mesh.devices.reshape(4, 16, 4, 2), ("x", "z", "y", "c"))
    placed = (
        P(DP, None),
        P(DP, None),
        P(DP, None),
        P(DP),
        P(None, MP),
        P(MP, None),
        P(DP + MP, None),
        P(DP + MP),
    )
    return jax.shard_map(
        body,
        mesh=split,
        in_specs=placed,
        out_specs=(P(None, MP), P(MP, None), P(DP + MP, None), P(DP + MP)),
        check_vma=False,
    )
```

time: 802 us -> 127 us (0.16)
  the two profiles are of different devices: /device:TPU:1 before, /device:TPU:32 now
where the time goes in v1:
time: 127 us; the launch traced here: 126 us
  blocking collectives  68 us (54%)
  waiting for transfers between devices  26.3 us (21%)
  starting transfers between devices  12.9 us (10%)
  local copies, waits for them, and re-layouts  8.19 us (6%)
  matrix products  5.88 us (5%)
  between operations  3.39 us (3%)
  other arithmetic  1.46 us (1%)
    all_to_all x1, blocking collectives, body(): buf = jnp.sum(lax.all_to_all(buf, 'z', 0, 0, tiled=True), axis=0)  30 us
    all_to_all x1, blocking collectives, body(): lax.all_to_all(buf, 'x', 0, 0, tiled=True)  16.1 us
    all_gather x1, blocking collectives, body(): full = lax.all_gather(full, 'x', tiled=False)  14.2 us
    all_to_all x1, waiting for transfers between devices, body(): full = lax.all_to_all(full, 'z', 0, 0, tiled=True)  12.6 us
    all_to_all x1, waiting for transfers between devices, body(): head_part = lax.all_to_all(head_part, MP, 0, 0, tiled=True)  8.49 us
    all_to_all x1, blocking collectives, body(): row_grad = lax.all_to_all(mine, MP, 0, 0, tiled=True).reshape(1, width)  7.64 us
    dot_general x13, matrix products, dot(): lax.dot_general(left, right, ((dims[:1], dims[1:]), ((), ())), precision=...  5.88 us
    all_to_all x1, waiting for transfers between devices, body(): lax.all_to_all(stats, MP, 0, 0, tiled=True)  5.23 us
  transfers between devices with their start and end apart: 3, of which 3 were waited for; matrix products, arithmetic and copies ran while one was open for 2% of the time, Pallas kernels for 0%

profile of v1, /device:TPU:32, one launch (start us, length us, event | category | flops | bytes accessed | tf_op | source)
XLA Modules:
  0.0 126.1 jit_solution(9632413507215677784)
XLA Ops:
  0.6 1.0 copy-done
  1.7 1.7 %fusion.3 = (f32[256,256]{0,1:T(8,128)S(1)}, f32[256,256]{0,1:T(8,128)S(1)}) fusion(f32[256,512]{1,0:T(8,128)} %param.8, f32[512,256]{1,0:T(8,128)S(1)} %copy-done), kind=kOutput, calls=%fused_computation.12 | convolution fusion | flops 201588736 | bytes 1572864 | tf_op jit(solution)/shard_map/dot_general | solution.py:14
  3.7 0.6 copy-done.3
  4.7 0.7 copy-done.6
  5.7 0.6 broadcast_in_dim.7
  6.3 4.5 %all-to-all-start = ((f32[8,8,128]{2,1,0:T(8,128)}), f32[8,8,128]{2,1,0:T(8,128)S(1)}, u32[]{:S(2)}, u32[]{:S(2)}) async-start(f32[8,8,128]{2,1,0:T(8,128)} %broadcast_in_dim.7), calls=%async_computation | async-start | bytes 65536 | tf_op jit(solution)/shard_map/all_to_all | solution.py:44
  11.0 5.2 %all-to-all-done = f32[8,8,128]{2,1,0:T(8,128)S(1)} async-done(((f32[8,8,128]{2,1,0:T(8,128)}), f32[8,8,128]{2,1,0:T(8,128)S(1)}, u32[]{:S(2)}, u32[]{:S(2)}) %all-to-all-start) | async-done | bytes 32800 | tf_op jit(solution)/shard_map/all_to_all | solution.py:44
  17.5 0.7 convolution_bitcast_fusion
  18.2 1.0 copy.45
  19.2 3.5 %all-to-all-start.1 = ((f32[8,64,256]{2,1,0:T(8,128)}), f32[8,64,256]{2,1,0:T(8,128)S(1)}, u32[]{:S(2)}, u32[]{:S(2)}) async-start(f32[8,64,256]{2,1,0:T(8,128)} %bitcast.15), calls=%async_computation.1 | async-start | bytes 1048576 | tf_op jit(solution)/shard_map/all_to_all | solution.py:63
  23.1 0.7 copy-done.2
  24.4 8.5 %all-to-all-done.1 = f32[8,64,256]{2,1,0:T(8,128)S(1)} async-done(((f32[8,64,256]{2,1,0:T(8,128)}), f32[8,64,256]{2,1,0:T(8,128)S(1)}, u32[]{:S(2)}, u32[]{:S(2)}) %all-to-all-start.1) | async-done | bytes 524320 | tf_op jit(solution)/shard_map/all_to_all | solution.py:63
  33.7 16.1 %all_to_all.34 = f32[4,384,128]{2,1,0:T(8,128)S(1)} all-to-all(f32[4,384,128]{2,1,0:T(8,128)S(1)} %bitcast.78), channel_id=1, replica_groups=mesh['x'=4,'z'=16,'y'=4,'c'=2] {'x'}, dimensions={0} | all-to-all | bytes 1572864 | tf_op jit(solution)/shard_map/all_to_all | solution.py:80
  49.9 30.0 %all_to_all.35 = f32[16,24,128]{2,1,0:T(8,128)S(1)} all-to-all(f32[16,24,128]{2,1,0:T(8,128)S(1)} %bitcast.82), channel_id=1, replica_groups=mesh['x'=4,'z'=16,'y'=4,'c'=2] {'z'}, dimensions={0} | all-to-all | bytes 393216 | tf_op jit(solution)/shard_map/all_to_all | solution.py:81
  80.0 7.6 %all_to_all.36 = f32[8,1,64]{2,1,0:T(1,128)S(1)} all-to-all(f32[8,1,64]{2,1,0:T(1,128)S(1)} %bitcast.89), channel_id=1, replica_groups=mesh['x'=4,'z'=16,'y'=4,'c'=2] {'y','c'}, dimensions={0} | all-to-all | bytes 4096 | tf_op jit(solution)/shard_map/all_to_all | solution.py:83
  87.6 0.7 broadcast_in_dim.8
  88.3 4.9 %all-to-all-start.4 = ((f32[16,24,128]{2,1,0:T(8,128)}), f32[16,24,128]{2,1,0:T(8,128)S(1)}, u32[]{:S(2)}, u32[]{:S(2)}) async-start(f32[16,24,128]{2,1,0:T(8,128)} %broadcast_in_dim.8), calls=%async_computation.4 | async-start | bytes 393216 | tf_op jit(solution)/shard_map/all_to_all | solution.py:87
  93.9 0.6 multiply_reduce_fusion.3
  95.3 0.6 copy-done.5
  95.9 0.6 sub.63
  96.5 12.6 %all-to-all-done.4 = f32[16,24,128]{2,1,0:T(8,128)S(1)} async-done(((f32[16,24,128]{2,1,0:T(8,128)}), f32[16,24,128]{2,1,0:T(8,128)S(1)}, u32[]{:S(2)}, u32[]{:S(2)}) %all-to-all-start.4) | async-done | bytes 196640 | tf_op jit(solution)/shard_map/all_to_all | solution.py:87
  109.1 14.2 %all-gather = f32[64,24,128]{2,1,0:T(8,128)S(1)} all-gather(f32[16,24,128]{2,1,0:T(8,128)S(1)} %all-to-all-done.4), channel_id=2, replica_groups=mesh['x'=4,'z'=16,'y'=4,'c'=2] {'x'}, dimensions={0}, use_global_device_ids=true | all-gather | bytes 983040 | tf_op jit(solution)/shard_map/all_gather | solution.py:88
  123.3 0.8 slice.53
  124.3 0.7 copy.57
  (46 shorter events, 4.6 us)
Async XLA Ops:
  0.6 1.0 copy-start
  1.7 2.0 %copy-start.1 = (f32[256,512]{1,0:T(8,128)S(1)}, f32[256,512]{1,0:T(8,128)}, u32[]{:S(2)}) copy-start(f32[256,512]{1,0:T(8,128)} %param.9) | copy-start | bytes 1572868
  3.4 0.9 copy-start.3
  4.7 0.7 copy-start.6
  6.3 9.9 %all-to-all-start = ((f32[8,8,128]{2,1,0:T(8,128)}), f32[8,8,128]{2,1,0:T(8,128)S(1)}, u32[]{:S(2)}, u32[]{:S(2)}) async-start(f32[8,8,128]{2,1,0:T(8,128)} %broadcast_in_dim.7), calls=%async_computation | async-start | bytes 65536 | tf_op jit(solution)/shard_map/all_to_all | solution.py:44
  19.2 13.7 %all-to-all-start.1 = ((f32[8,64,256]{2,1,0:T(8,128)}), f32[8,64,256]{2,1,0:T(8,128)S(1)}, u32[]{:S(2)}, u32[]{:S(2)}) async-start(f32[8,64,256]{2,1,0:T(8,128)} %bitcast.15), calls=%async_computation.1 | async-start | bytes 1048576 | tf_op jit(solution)/shard_map/all_to_all | solution.py:63
  22.7 1.0 copy-start.2
  24.4 8.5 %copy-start.4 = (s32[256]{0:T(256)S(1)}, s32[256]{0:T(256)}, u32[]{:S(2)}) copy-start(s32[256]{0:T(256)} %param.11) | copy-start | bytes 3076
  88.3 20.7 %all-to-all-start.4 = ((f32[16,24,128]{2,1,0:T(8,128)}), f32[16,24,128]{2,1,0:T(8,128)S(1)}, u32[]{:S(2)}, u32[]{:S(2)}) async-start(f32[16,24,128]{2,1,0:T(8,128)} %broadcast_in_dim.8), calls=%async_computation.4 | async-start | bytes 393216 | tf_op jit(solution)/shard_map/all_to_all | solution.py:87
  95.2 0.7 copy-start.5

commit v2 on v1

--- a/solution.py
+++ b/solution.py
@@ -79,8 +79,10 @@
     buf = jnp.concatenate([w1c, w2c, slab], axis=2).reshape(n_x, n_z * 24, 128)
     buf = jnp.sum(lax.all_to_all(buf, "x", 0, 0, tiled=True), axis=0).reshape(n_z, 24, 128)
     buf = jnp.sum(lax.all_to_all(buf, "z", 0, 0, tiled=True), axis=0)
-    mine = buf[20:].reshape(half, 2, fblk).transpose(1, 0, 2).reshape(n_mp, fblk)
-    row_grad = lax.all_to_all(mine, MP, 0, 0, tiled=True).reshape(1, width)
+    mine = lax.all_gather(buf[20:], MP, tiled=False)
+    mine = mine.reshape(n_mp, half, 2, fblk)
+    who = lax.axis_index(MP)
+    row_grad = lax.dynamic_slice(mine, (0, who % half, who // half, 0), (n_mp, 1, 1, fblk)).reshape(1, width)
     new_accum = accum + jnp.sum(row_grad * row_grad, axis=1) / width
     new_table = table - 0.5 * row_grad * lax.rsqrt(new_accum)[:, None]
     full = jnp.broadcast_to(buf[None], (n_z, 24, 128))

time: 127 us -> 118 us (0.929)
  waiting for transfers between devices: 26.3 us -> 13.7 us
  blocking collectives: 68 us -> 71.8 us
    all_to_all x1, waiting for transfers between devices: 12.6 us -> 0.01 us  [body(): full = lax.all_to_all(full, 'z', 0, 0, tiled=True)]
    all_gather x0 -> x1, blocking collectives: none -> 11.3 us  [body(): mine = lax.all_gather(buf[20:], MP, tiled=False)]
    all_to_all x1 -> x0, blocking collectives: 7.64 us -> none  [body(): row_grad = lax.all_to_all(mine, MP, 0, 0, tiled=True).reshape(1, width)]
    unnamed x16 -> x17, local copies, waits for them, and re-layouts: 4.31 us -> 4.31 us
  transfers between devices with their start and end apart: 3 -> 3, of which waited for: 3 -> 2; matrix products, arithmetic and copies ran while one was open for 2% -> 2% of each run, Pallas kernels for 0% -> 0%
where the time goes in v2:
time: 118 us; the launch traced here: 117 us
  blocking collectives  71.8 us (61%)
  waiting for transfers between devices  13.7 us (12%)
  starting transfers between devices  12.9 us (11%)
  local copies, waits for them, and re-layouts  8.2 us (7%)
  matrix products  5.88 us (5%)
  between operations  3.4 us (3%)
  other arithmetic  1.48 us (1%)
    all_to_all x1, blocking collectives, body(): buf = jnp.sum(lax.all_to_all(buf, 'z', 0, 0, tiled=True), axis=0)  30 us
    all_to_all x1, blocking collectives, body(): lax.all_to_all(buf, 'x', 0, 0, tiled=True)  16.1 us
    all_gather x1, blocking collectives, body(): full = lax.all_gather(full, 'x', tiled=False)  14.5 us
    all_gather x1, blocking collectives, body(): mine = lax.all_gather(buf[20:], MP, tiled=False)  11.3 us
    all_to_all x1, waiting for transfers between devices, body(): head_part = lax.all_to_all(head_part, MP, 0, 0, tiled=True)  8.49 us
    dot_general x13, matrix products, dot(): lax.dot_general(left, right, ((dims[:1], dims[1:]), ((), ())), precision=...  5.88 us
    all_to_all x1, waiting for transfers between devices, body(): lax.all_to_all(stats, MP, 0, 0, tiled=True)  5.23 us
    all_to_all x1, starting transfers between devices, body(): full = lax.all_to_all(full, 'z', 0, 0, tiled=True)  4.94 us
  transfers between devices with their start and end apart: 3, of which 2 were waited for; matrix products, arithmetic and copies ran while one was open for 2% of the time, Pallas kernels for 0%

profile of v2, /device:TPU:32, one launch (start us, length us, event | category | flops | bytes accessed | tf_op | source)
XLA Modules:
  0.0 117.4 jit_solution(7439271321943562842)
XLA Ops:
  0.6 1.0 copy-done
  1.7 1.7 %fusion.3 = (f32[256,256]{0,1:T(8,128)S(1)}, f32[256,256]{0,1:T(8,128)S(1)}) fusion(f32[256,512]{1,0:T(8,128)} %param.8, f32[512,256]{1,0:T(8,128)S(1)} %copy-done), kind=kOutput, calls=%fused_computation.12 | convolution fusion | flops 201588736 | bytes 1572864 | tf_op jit(solution)/shard_map/dot_general | solution.py:14
  3.7 0.6 copy-done.3
  4.7 0.7 copy-done.6
  5.7 0.6 broadcast_in_dim.7
  6.3 4.5 %all-to-all-start = ((f32[8,8,128]{2,1,0:T(8,128)}), f32[8,8,128]{2,1,0:T(8,128)S(1)}, u32[]{:S(2)}, u32[]{:S(2)}) async-start(f32[8,8,128]{2,1,0:T(8,128)} %broadcast_in_dim.7), calls=%async_computation | async-start | bytes 65536 | tf_op jit(solution)/shard_map/all_to_all | solution.py:44
  11.0 5.2 %all-to-all-done = f32[8,8,128]{2,1,0:T(8,128)S(1)} async-done(((f32[8,8,128]{2,1,0:T(8,128)}), f32[8,8,128]{2,1,0:T(8,128)S(1)}, u32[]{:S(2)}, u32[]{:S(2)}) %all-to-all-start) | async-done | bytes 32800 | tf_op jit(solution)/shard_map/all_to_all | solution.py:44
  17.5 0.7 convolution_bitcast_fusion
  18.2 1.0 copy.43
  19.2 3.5 %all-to-all-start.1 = ((f32[8,64,256]{2,1,0:T(8,128)}), f32[8,64,256]{2,1,0:T(8,128)S(1)}, u32[]{:S(2)}, u32[]{:S(2)}) async-start(f32[8,64,256]{2,1,0:T(8,128)} %bitcast.15), calls=%async_computation.1 | async-start | bytes 1048576 | tf_op jit(solution)/shard_map/all_to_all | solution.py:63
  23.1 0.7 copy-done.2
  23.7 0.5 convolution_bitcast_fusion.1
  24.4 8.5 %all-to-all-done.1 = f32[8,64,256]{2,1,0:T(8,128)S(1)} async-done(((f32[8,64,256]{2,1,0:T(8,128)}), f32[8,64,256]{2,1,0:T(8,128)S(1)}, u32[]{:S(2)}, u32[]{:S(2)}) %all-to-all-start.1) | async-done | bytes 524320 | tf_op jit(solution)/shard_map/all_to_all | solution.py:63
  33.7 16.1 %all_to_all.25 = f32[4,384,128]{2,1,0:T(8,128)S(1)} all-to-all(f32[4,384,128]{2,1,0:T(8,128)S(1)} %bitcast.78), channel_id=1, replica_groups=mesh['x'=4,'z'=16,'y'=4,'c'=2] {'x'}, dimensions={0} | all-to-all | bytes 1572864 | tf_op jit(solution)/shard_map/all_to_all | solution.py:80
  49.9 30.0 %all_to_all.26 = f32[16,24,128]{2,1,0:T(8,128)S(1)} all-to-all(f32[16,24,128]{2,1,0:T(8,128)S(1)} %bitcast.82), channel_id=1, replica_groups=mesh['x'=4,'z'=16,'y'=4,'c'=2] {'z'}, dimensions={0} | all-to-all | bytes 393216 | tf_op jit(solution)/shard_map/all_to_all | solution.py:81
  79.9 0.7 broadcast_in_dim.8
  80.6 4.9 %all-to-all-start.4 = ((f32[16,24,128]{2,1,0:T(8,128)}), f32[16,24,128]{2,1,0:T(8,128)S(1)}, u32[]{:S(2)}, u32[]{:S(2)}) async-start(f32[16,24,128]{2,1,0:T(8,128)} %broadcast_in_dim.8), calls=%async_computation.4 | async-start | bytes 393216 | tf_op jit(solution)/shard_map/all_to_all | solution.py:89
  86.2 11.3 %all-gather.2 = f32[8,4,128]{2,1,0:T(4,128)S(1)} all-gather(f32[1,4,128]{2,1,0:T(4,128)S(1)} %slice_bitcast_fusion.1), channel_id=3, replica_groups=mesh['x'=4,'z'=16,'y'=4,'c'=2] {'y','c'}, dimensions={0}, use_global_device_ids=true | all-gather | bytes 18432 | tf_op jit(solution)/shard_map/all_gather | solution.py:82
  97.6 0.6 multiply_reduce_fusion.3
  99.0 0.6 copy-done.5
  99.6 0.6 sub.68
  100.2 14.5 %all-gather = f32[64,24,128]{2,1,0:T(8,128)S(1)} all-gather(f32[16,24,128]{2,1,0:T(8,128)S(1)} %all-to-all-done.4), channel_id=2, replica_groups=mesh['x'=4,'z'=16,'y'=4,'c'=2] {'x'}, dimensions={0}, use_global_device_ids=true | all-gather | bytes 983040 | tf_op jit(solution)/shard_map/all_gather | solution.py:90
  114.7 0.8 slice.53
  115.6 0.7 copy.54
  (46 shorter events, 4.1 us)
Async XLA Ops:
  0.6 1.0 copy-start
  1.7 2.0 %copy-start.1 = (f32[256,512]{1,0:T(8,128)S(1)}, f32[256,512]{1,0:T(8,128)}, u32[]{:S(2)}) copy-start(f32[256,512]{1,0:T(8,128)} %param.9) | copy-start | bytes 1572868
  3.4 0.9 copy-start.3
  4.7 0.7 copy-start.6
  6.3 9.9 %all-to-all-start = ((f32[8,8,128]{2,1,0:T(8,128)}), f32[8,8,128]{2,1,0:T(8,128)S(1)}, u32[]{:S(2)}, u32[]{:S(2)}) async-start(f32[8,8,128]{2,1,0:T(8,128)} %broadcast_in_dim.7), calls=%async_computation | async-start | bytes 65536 | tf_op jit(solution)/shard_map/all_to_all | solution.py:44
  19.2 13.7 %all-to-all-start.1 = ((f32[8,64,256]{2,1,0:T(8,128)}), f32[8,64,256]{2,1,0:T(8,128)S(1)}, u32[]{:S(2)}, u32[]{:S(2)}) async-start(f32[8,64,256]{2,1,0:T(8,128)} %bitcast.15), calls=%async_computation.1 | async-start | bytes 1048576 | tf_op jit(solution)/shard_map/all_to_all | solution.py:63
  22.7 1.0 copy-start.2
  24.4 8.5 %copy-start.4 = (s32[256]{0:T(256)S(1)}, s32[256]{0:T(256)}, u32[]{:S(2)}) copy-start(s32[256]{0:T(256)} %param.11) | copy-start | bytes 3076
  80.6 19.6 %all-to-all-start.4 = ((f32[16,24,128]{2,1,0:T(8,128)}), f32[16,24,128]{2,1,0:T(8,128)S(1)}, u32[]{:S(2)}, u32[]{:S(2)}) async-start(f32[16,24,128]{2,1,0:T(8,128)} %broadcast_in_dim.8), calls=%async_computation.4 | async-start | bytes 393216 | tf_op jit(solution)/shard_map/all_to_all | solution.py:89
  98.9 0.7 copy-start.5

commit v3 on v2

--- a/solution.py
+++ b/solution.py
@@ -7,7 +7,8 @@
 HEAD_DIM = 64
 HIGH = lax.Precision.HIGH
 MP = ("y", "c")
-DP = ("x", "z")
+DP = ("x", "h", "l")
+XL = ("x", "l")
 
 
 def dot(left, right, dims):
@@ -21,7 +22,8 @@
     count, width = layer_input.shape
     hd = HEAD_DIM
     scale = hd ** (-0.5)
-    n_x, n_z = lax.axis_size("x"), lax.axis_size("z")
+    n_x, n_h, n_l = lax.axis_size("x"), lax.axis_size("h"), lax.axis_size("l")
+    n_xl = n_x * n_l
     n_mp = lax.axis_size(MP)
     pre = dot(layer_input, w_uvqk, (1, 0))
     psig = jax.nn.sigmoid(pre)
@@ -64,37 +66,39 @@
     fblk = width // n_mp
     own = lax.dynamic_slice(grad_out, (0, lax.axis_index(MP) * fblk), (count, fblk))
     xgrad = jnp.sum(head_part, axis=0).T + own
-    rows = n_x * n_z * n_mp
     half = n_mp // 2
-    ids = jnp.arange(rows // 2, dtype=jnp.int32)
-    target = (ids // half) * n_mp + ids % half
+    ids = jnp.arange(n_xl * n_h * half, dtype=jnp.int32)
+    piece = ids // (n_h * half)
+    owner = (piece // n_l) * (n_h * n_l) + (ids // half % n_h) * n_l + piece % n_l
+    target = owner * n_mp + ids % half
     slab = jnp.concatenate([
         dot((t[:, None] == item_ids[None, :]).astype(jnp.float32), xgrad, (1, 0))
         for t in (target, target + half)
-    ], axis=1).reshape(n_x, n_z, half, 2 * fblk)
+    ], axis=1).reshape(n_xl, n_h * half, 2 * fblk)
     w1 = dot(layer_input, dpre, (0, 0))
     w2 = dot(zval, grad_out, (0, 0))
-    w1c = w1.reshape(n_x, n_z, 8, 2, 128).transpose(0, 1, 3, 2, 4).reshape(n_x, n_z, 16, 128)
-    w2c = w2.reshape(n_z, 4, n_x, 128).transpose(2, 0, 1, 3)
-    buf = jnp.concatenate([w1c, w2c, slab], axis=2).reshape(n_x, n_z * 24, 128)
-    buf = jnp.sum(lax.all_to_all(buf, "x", 0, 0, tiled=True), axis=0).reshape(n_z, 24, 128)
-    buf = jnp.sum(lax.all_to_all(buf, "z", 0, 0, tiled=True), axis=0)
-    mine = lax.all_gather(buf[20:], MP, tiled=False)
+    w1c = w1.reshape(n_xl, 4, 8, 2, 128).transpose(0, 1, 3, 2, 4).reshape(n_xl, 64, 128)
+    w2c = w2.reshape(n_l, 16, n_x, 128).transpose(2, 0, 1, 3).reshape(n_xl, 16, 128)
+    buf = jnp.concatenate([w1c, w2c, slab], axis=1)
+    buf = jnp.sum(lax.all_to_all(buf, XL, 0, 0, tiled=True), axis=0)
+    buf = jnp.broadcast_to(buf[None], (n_h, 96, 128))
+    buf = jnp.sum(lax.all_to_all(buf, "h", 0, 0, tiled=True), axis=0)
+    full = jnp.broadcast_to(buf[None, :80], (n_xl, 80, 128))
+    full = lax.all_to_all(full, XL, 0, 0, tiled=True)
+    w1g = full[:, :64].reshape(n_xl, 4, 2, 8, 128).transpose(0, 1, 3, 2, 4).reshape(width, 4 * hd)
+    w2g = full[:, 64:].reshape(n_x, n_l, 16, 128).transpose(1, 2, 0, 3).reshape(hd, width)
+    mine = lax.dynamic_slice(buf, (80 + half * lax.axis_index("h"), 0), (half, 128))
+    mine = lax.all_gather(mine, MP, tiled=False)
     mine = mine.reshape(n_mp, half, 2, fblk)
     who = lax.axis_index(MP)
     row_grad = lax.dynamic_slice(mine, (0, who % half, who // half, 0), (n_mp, 1, 1, fblk)).reshape(1, width)
     new_accum = accum + jnp.sum(row_grad * row_grad, axis=1) / width
     new_table = table - 0.5 * row_grad * lax.rsqrt(new_accum)[:, None]
-    full = jnp.broadcast_to(buf[None], (n_z, 24, 128))
-    full = lax.all_to_all(full, "z", 0, 0, tiled=True)
-    full = lax.all_gather(full, "x", tiled=False)
-    w1g = full[:, :, :16].reshape(n_x, n_z, 2, 8, 128).transpose(0, 1, 3, 2, 4).reshape(width, 4 * hd)
-    w2g = full[:, :, 16:20].transpose(1, 2, 0, 3).reshape(hd, width)
     return (w1g, w2g, new_table, new_accum)
 
 
 def solution(mesh):
-    split = Mesh(mesh.devices.reshape(4, 16, 4, 2), ("x", "z", "y", "c"))
+    split = Mesh(mesh.devices.reshape(4, 4, 4, 4, 2), ("x", "h", "l", "y", "c"))
     placed = (
         P(DP, None),
         P(DP, None),

time: 118 us -> 118 us (level)
  the two profiles are of different devices: /device:TPU:32 before, /device:TPU:1 now
where the time goes in v3:
time: 118 us
  blocking collectives  66.4 us (56%)
  starting transfers between devices  19.1 us (16%)
  waiting for transfers between devices  12.2 us (10%)
  local copies, waits for them, and re-layouts  9.08 us (8%)
  matrix products  5.88 us (5%)
  between operations  3.41 us (3%)
  other arithmetic  1.46 us (1%)
    all_to_all x1, blocking collectives, body(): buf = jnp.sum(lax.all_to_all(buf, 'h', 0, 0, tiled=True), axis=0)  26.2 us
    all_to_all x1, blocking collectives, body(): buf = jnp.sum(lax.all_to_all(buf, XL, 0, 0, tiled=True), axis=0)  25.4 us
    all_gather x1, blocking collectives, body(): mine = lax.all_gather(mine, MP, tiled=False)  14.9 us
    all_to_all x1, starting transfers between devices, body(): lax.all_to_all(stats, MP, 0, 0, tiled=True)  10.1 us
    all_to_all x1, waiting for transfers between devices, body(): head_part = lax.all_to_all(head_part, MP, 0, 0, tiled=True)  7.64 us
    dot_general x13, matrix products, dot(): lax.dot_general(left, right, ((dims[:1], dims[1:]), ((), ())), precision=...  5.88 us
    unnamed x17, local copies, waits for them, and re-layouts  5.01 us
    all_to_all x1, starting transfers between devices, body(): full = lax.all_to_all(full, XL, 0, 0, tiled=True)  4.93 us
  transfers between devices with their start and end apart: 3, of which 2 were waited for; matrix products, arithmetic and copies ran while one was open for 2% of the time, Pallas kernels for 0%

profile of v3, /device:TPU:1, one launch (start us, length us, event | category | flops | bytes accessed | tf_op | source)
XLA Modules:
  0.0 117.6 jit_solution(2700445689807495695)
XLA Ops:
  0.6 1.0 copy-done
  1.7 1.7 %fusion.3 = (f32[256,256]{0,1:T(8,128)S(1)}, f32[256,256]{0,1:T(8,128)S(1)}) fusion(f32[256,512]{1,0:T(8,128)} %param.8, f32[512,256]{1,0:T(8,128)S(1)} %copy-done), kind=kOutput, calls=%fused_computation.12 | convolution fusion | flops 201588736 | bytes 1572864 | tf_op jit(solution)/shard_map/dot_general | solution.py:15
  3.7 0.6 copy-done.3
  4.7 0.7 copy-done.6
  5.7 0.6 broadcast_in_dim.9
  6.3 10.1 %all-to-all-start = ((f32[8,8,128]{2,1,0:T(8,128)}), f32[8,8,128]{2,1,0:T(8,128)S(1)}, u32[]{:S(2)}, u32[]{:S(2)}) async-start(f32[8,8,128]{2,1,0:T(8,128)} %broadcast_in_dim.9), calls=%async_computation | async-start | bytes 65536 | tf_op jit(solution)/shard_map/all_to_all | solution.py:46
  16.6 4.5 %all-to-all-done = f32[8,8,128]{2,1,0:T(8,128)S(1)} async-done(((f32[8,8,128]{2,1,0:T(8,128)}), f32[8,8,128]{2,1,0:T(8,128)S(1)}, u32[]{:S(2)}, u32[]{:S(2)}) %all-to-all-start) | async-done | bytes 32800 | tf_op jit(solution)/shard_map/all_to_all | solution.py:46
  22.4 0.7 convolution_bitcast_fusion
  23.1 1.0 copy.41
  24.1 4.1 %all-to-all-start.1 = ((f32[8,64,256]{2,1,0:T(8,128)}), f32[8,64,256]{2,1,0:T(8,128)S(1)}, u32[]{:S(2)}, u32[]{:S(2)}) async-start(f32[8,64,256]{2,1,0:T(8,128)} %bitcast.16), calls=%async_computation.1 | async-start | bytes 1048576 | tf_op jit(solution)/shard_map/all_to_all | solution.py:65
  28.6 0.7 copy-done.2
  29.3 0.5 convolution_bitcast_fusion.1
  30.0 7.6 %all-to-all-done.1 = f32[8,64,256]{2,1,0:T(8,128)S(1)} async-done(((f32[8,64,256]{2,1,0:T(8,128)}), f32[8,64,256]{2,1,0:T(8,128)S(1)}, u32[]{:S(2)}, u32[]{:S(2)}) %all-to-all-start.1) | async-done | bytes 524320 | tf_op jit(solution)/shard_map/all_to_all | solution.py:65
  37.6 0.7 copy-done.4
  39.1 25.4 %all_to_all.25 = f32[16,96,128]{2,1,0:T(8,128)S(1)} all-to-all(f32[16,96,128]{2,1,0:T(8,128)S(1)} %pad_maximum_fusion), channel_id=1, replica_groups=mesh['x'=4,'h'=4,'l'=4,'y'=4,'c'=2] {'x','l'}, dimensions={0} | all-to-all | bytes 1572864 | tf_op jit(solution)/shard_map/all_to_all | solution.py:83
  64.5 26.2 %all_to_all.26 = f32[4,96,128]{2,1,0:T(8,128)S(1)} all-to-all(f32[4,96,128]{2,1,0:T(8,128)S(1)} %broadcast_in_dim.10), channel_id=1, replica_groups=mesh['x'=4,'h'=4,'l'=4,'y'=4,'c'=2] {'h'}, dimensions={0} | all-to-all | bytes 393216 | tf_op jit(solution)/shard_map/all_to_all | solution.py:85
  90.7 0.9 broadcast_in_dim.11
  91.6 4.9 %all-to-all-start.4 = ((f32[16,80,128]{2,1,0:T(8,128)}), f32[16,80,128]{2,1,0:T(8,128)S(1)}, u32[]{:S(2)}, u32[]{:S(2)}) async-start(f32[16,80,128]{2,1,0:T(8,128)} %broadcast_in_dim.11), calls=%async_computation.4 | async-start | bytes 1310720 | tf_op jit(solution)/shard_map/all_to_all | solution.py:87
  97.2 14.9 %all-gather.1 = f32[8,4,128]{2,1,0:T(4,128)S(1)} all-gather(f32[1,4,128]{2,1,0:T(4,128)S(1)} %dynamic-slice_bitcast_fusion), channel_id=2, replica_groups=mesh['x'=4,'h'=4,'l'=4,'y'=4,'c'=2] {'y','c'}, dimensions={0}, use_global_device_ids=true | all-gather | bytes 18432 | tf_op jit(solution)/shard_map/all_gather | solution.py:91
  112.2 0.6 multiply_reduce_fusion.3
  113.7 0.6 copy-done.5
  114.3 0.6 sub.82
  114.9 0.7 copy.51
  115.6 0.8 slice.54
  (46 shorter events, 4.1 us)
Async XLA Ops:
  0.6 1.0 copy-start
  1.7 2.0 %copy-start.1 = (f32[256,512]{1,0:T(8,128)S(1)}, f32[256,512]{1,0:T(8,128)}, u32[]{:S(2)}) copy-start(f32[256,512]{1,0:T(8,128)} %param.9) | copy-start | bytes 1572868
  3.4 0.9 copy-start.3
  4.7 0.7 copy-start.6
  6.3 14.8 %all-to-all-start = ((f32[8,8,128]{2,1,0:T(8,128)}), f32[8,8,128]{2,1,0:T(8,128)S(1)}, u32[]{:S(2)}, u32[]{:S(2)}) async-start(f32[8,8,128]{2,1,0:T(8,128)} %broadcast_in_dim.9), calls=%async_computation | async-start | bytes 65536 | tf_op jit(solution)/shard_map/all_to_all | solution.py:46
  24.1 13.5 %all-to-all-start.1 = ((f32[8,64,256]{2,1,0:T(8,128)}), f32[8,64,256]{2,1,0:T(8,128)S(1)}, u32[]{:S(2)}, u32[]{:S(2)}) async-start(f32[8,64,256]{2,1,0:T(8,128)} %bitcast.16), calls=%async_computation.1 | async-start | bytes 1048576 | tf_op jit(solution)/shard_map/all_to_all | solution.py:65
  28.2 1.0 copy-start.2
  37.6 0.7 copy-start.4
  91.6 23.3 %all-to-all-start.4 = ((f32[16,80,128]{2,1,0:T(8,128)}), f32[16,80,128]{2,1,0:T(8,128)S(1)}, u32[]{:S(2)}, u32[]{:S(2)}) async-start(f32[16,80,128]{2,1,0:T(8,128)} %broadcast_in_dim.11), calls=%async_computation.4 | async-start | bytes 1310720 | tf_op jit(solution)/shard_map/all_to_all | solution.py:87
  113.6 0.7 copy-start.5

commit v4 on v3

v4 whole, which is shorter than its diff:
```python
import functools

import jax
import jax.numpy as jnp
from jax import lax
from jax.experimental import pallas as pl
from jax.experimental.pallas import tpu as pltpu
from jax.sharding import Mesh
from jax.sharding import PartitionSpec as P

HEAD_DIM = 64
MP = ("y", "c")
DP = ("x", "h", "l")
XL = ("x", "l")


def mm(left, right, dims):
    return lax.dot_general(
        left, right, ((dims[:1], dims[1:]), ((), ())),
        preferred_element_type=jnp.float32,
    )


def halves(value):
    high = value.astype(jnp.bfloat16)
    return high, (value - high.astype(jnp.float32)).astype(jnp.bfloat16)


def dot(left, right, dims):
    lh, ll = halves(left)
    rh, rl = halves(right)
    return mm(lh, rh, dims) + (mm(lh, rl, dims) + mm(ll, rh, dims))


def forward(*refs):
    sources, outs, held, sems = refs[:5], refs[5:11], refs[11:16], refs[16]
    copies = [
        pltpu.make_async_copy(source, target, sems.at[i])
        for i, (source, target) in enumerate(zip(sources, held))
    ]
    for copy in copies:
        copy.start()
    x_ref, w_ref, g_ref, wo_ref, seg_ref = held
    act_ref, dfac_ref, attn_ref, dsf_ref, od_ref, stats_ref = outs
    count = x_ref.shape[0]
    copies[0].wait()
    copies[1].wait()
    hd = HEAD_DIM
    scale = hd ** (-0.5)
    pre = dot(x_ref[...], w_ref[...], (1, 0))
    psig = jax.nn.sigmoid(pre)
    act = pre * psig
    act_ref[...] = act
    dfac_ref[...] = psig * (1.0 + pre * (1.0 - psig))
    ublk, vblk, qblk, kblk = (act[:, i * hd:(i + 1) * hd] for i in range(4))
    copies[4].wait()
    seg = jnp.broadcast_to(seg_ref[...].astype(jnp.float32), (count, count))
    row = lax.broadcasted_iota(jnp.int32, (count, count), 0)
    col = lax.broadcasted_iota(jnp.int32, (count, count), 1)
    mask = jnp.logical_and(seg.T == seg, row >= col)
    score = dot(qblk, kblk, (1, 1)) * scale
    sigm = jax.nn.sigmoid(score)
    attn = jnp.where(mask, score * sigm, 0.0)
    attn_ref[...] = attn
    dsf_ref[...] = jnp.where(mask, sigm * (1.0 + score * (1.0 - sigm)) * scale, 0.0)
    outv = dot(attn, vblk, (1, 0))
    copies[2].wait()
    copies[3].wait()
    dzval = dot(g_ref[...], wo_ref[...], (1, 1))
    dnorm = dzval * ublk
    od_ref[...] = jnp.concatenate([outv, dzval], axis=1)
    terms = jnp.concatenate([outv, outv * outv, dnorm, dnorm * outv], axis=1)
    pick = lax.broadcasted_iota(jnp.int32, (8, 4 * hd), 0) & 3
    blk = lax.broadcasted_iota(jnp.int32, (8, 4 * hd), 1) >> 6
    ones = (pick == blk).astype(jnp.bfloat16)
    th, tl = halves(terms)
    sums = mm(ones, th, (1, 1)) + mm(ones, tl, (1, 1))
    upper = lax.broadcasted_iota(jnp.int32, (8, 128), 0) < 4
    packed = jnp.where(upper, sums[:, :128], sums[:, 128:])
    stats_ref[...] = jnp.broadcast_to(packed[None], stats_ref.shape)


def backward(width, st_ref, act_ref, dfac_ref, attn_ref, dsf_ref, od_ref, w_ref, dpre_ref, z_ref, part_ref):
    hd = HEAD_DIM
    sums = jnp.sum(st_ref[...], axis=0)
    wide = jnp.concatenate([sums, jnp.zeros((120, 128), jnp.float32)], axis=0).T

    def column(i):
        return jnp.concatenate([wide[:, i:i + 1], wide[:, i + 4:i + 5]], axis=0)

    mean = column(0) / width
    var = column(1) / width - mean * mean
    rstd = lax.rsqrt(var + 1e-05)
    first = column(2) / width
    second = rstd * (column(3) - mean * column(2)) / width
    act = act_ref[...]
    ublk, vblk, qblk, kblk = (act[:, i * hd:(i + 1) * hd] for i in range(4))
    outv, dzval = od_ref[:, :hd], od_ref[:, hd:]
    normed = (outv - mean) * rstd
    z_ref[...] = normed * ublk
    dnorm = dzval * ublk
    dout = rstd * (dnorm - first - normed * second)
    dattn = dot(dout, vblk, (1, 1))
    dvblk = dot(attn_ref[...], dout, (0, 0))
    dscore = dattn * dsf_ref[...]
    dqblk = dot(dscore, kblk, (1, 0))
    dkblk = dot(dscore, qblk, (0, 0))
    dpre = jnp.concatenate([dzval * normed, dvblk, dqblk, dkblk], axis=1) * dfac_ref[...]
    dpre_ref[...] = dpre
    part_ref[...] = dot(w_ref[...], dpre, (1, 1))


def packing(recv_ref, own_ref, ids_ref, w1_ref, w2_ref, buf_ref):
    xgrad = jnp.sum(recv_ref[...], axis=0) + own_ref[...]
    xh, xl = halves(xgrad)
    count = xgrad.shape[1]
    ids = jnp.broadcast_to(ids_ref[...], (256, count))
    spot = lax.broadcasted_iota(jnp.int32, (256, count), 0)
    piece = spot >> 4
    owner = ((piece >> 2) << 4) + (((spot >> 2) & 3) << 2) + (piece & 3)
    target = (owner << 3) + (spot & 3)
    sides = []
    for shift in (0, 4):
        hits = (ids == target + shift).astype(jnp.float32).astype(jnp.bfloat16)
        sides.append(mm(hits, xh, (1, 1)) + mm(hits, xl, (1, 1)))
    slab = jnp.concatenate(sides, axis=1)
    for n in range(16):
        for t in range(4):
            for a in range(2):
                buf_ref[n, t * 16 + a * 8:t * 16 + a * 8 + 8, :] = w1_ref[
                    n * 32 + t * 8:n * 32 + t * 8 + 8, a * 128:a * 128 + 128]
        x, l = n // 4, n % 4
        buf_ref[n, 64:80, :] = w2_ref[l * 16:l * 16 + 16, x * 128:x * 128 + 128]
        buf_ref[n, 80:96, :] = slab[n * 16:n * 16 + 16]


def call(kernel, *shapes, plain=(), loose=(), remote=None):
    extra = {}
    if remote:
        extra = dict(
            in_specs=[pl.BlockSpec(memory_space=pltpu.HBM) for _ in remote],
            scratch_shapes=[pltpu.VMEM(t.shape, t.dtype) for t in remote]
            + [pltpu.SemaphoreType.DMA((len(remote),))],
        )
    run = pl.pallas_call(
        kernel,
        out_shape=[
            jax.ShapeDtypeStruct(t, jnp.float32) if i in plain else pltpu.VMEM(t, jnp.float32)
            for i, t in enumerate(shapes)
        ],
        compiler_params=pltpu.CompilerParams(vmem_limit_bytes=16 << 20),
        **extra,
    )

    def with_vmem(*args):
        return run(*(
            pltpu.with_memory_space_constraint(t, pltpu.HBM if i in loose else pltpu.VMEM)
            for i, t in enumerate(args)
        ))
    return with_vmem


def body(layer_input, grad_out, segment, item_ids, w_uvqk, w_out, table, accum):
    count, width = layer_input.shape
    hd = HEAD_DIM
    n_x, n_h, n_l = lax.axis_size("x"), lax.axis_size("h"), lax.axis_size("l")
    n_xl = n_x * n_l
    n_mp = lax.axis_size(MP)
    fblk = width // n_mp
    half = n_mp // 2
    square = (count, count)
    given = (layer_input, w_uvqk, grad_out, w_out, segment)
    act, dfac, attn, dsf, od, stats = call(
        forward, (count, 4 * hd), (count, 4 * hd), square, square, (count, 2 * hd), (n_mp, 8, 128),
        plain=(5,), loose=(0, 1, 2, 3, 4), remote=given,
    )(*given)
    own = lax.dynamic_slice(grad_out, (0, lax.axis_index(MP) * fblk), (count, fblk)).T
    stats = lax.all_to_all(stats, MP, 0, 0, tiled=True)
    dpre, zval, part = call(
        functools.partial(backward, width), (count, 4 * hd), (count, hd), (width, count), plain=(2,),
    )(stats, act, dfac, attn, dsf, od, w_uvqk)
    part = lax.all_to_all(part.reshape(n_mp, fblk, count), MP, 0, 0, tiled=True)
    w1 = lax.dot_general(
        layer_input, dpre, (((0,), (0,)), ((), ())),
        precision=lax.Precision.HIGH, preferred_element_type=jnp.float32)
    w2 = lax.dot_general(
        zval, grad_out, (((0,), (0,)), ((), ())),
        precision=lax.Precision.HIGH, preferred_element_type=jnp.float32)
    buf, = call(packing, (n_xl, 96, 128))(part, own, item_ids.reshape(1, count), w1, w2)
    buf = jnp.sum(lax.all_to_all(buf, XL, 0, 0, tiled=True), axis=0)
    buf = jnp.broadcast_to(buf[None], (n_h, 96, 128))
    buf = jnp.sum(lax.all_to_all(buf, "h", 0, 0, tiled=True), axis=0)
    full = jnp.broadcast_to(buf[None, :80], (n_xl, 80, 128))
    full = lax.all_to_all(full, XL, 0, 0, tiled=True)
    w1g = full[:, :64].reshape(n_xl, 4, 2, 8, 128).transpose(0, 1, 3, 2, 4).reshape(width, 4 * hd)
    w2g = full[:, 64:].reshape(n_x, n_l, 16, 128).transpose(1, 2, 0, 3).reshape(hd, width)
    mine = lax.dynamic_slice(buf, (80 + half * lax.axis_index("h"), 0), (half, 128))
    mine = lax.all_gather(lax.all_gather(mine, "c", tiled=False), "y", tiled=False)
    mine = mine.reshape(n_mp, half, 2, fblk)
    who = lax.axis_index(MP)
    row_grad = lax.dynamic_slice(mine, (0, who % half, who // half, 0), (n_mp, 1, 1, fblk)).reshape(1, width)
    new_accum = accum + jnp.sum(row_grad * row_grad, axis=1) / width
    new_table = table - 0.5 * row_grad * lax.rsqrt(new_accum)[:, None]
    return (w1g, w2g, new_table, new_accum)


def solution(mesh):
    split = Mesh(mesh.devices.reshape(4, 4, 4, 4, 2), ("x", "h", "l", "y", "c"))
    placed = (
        P(DP, None),
        P(DP, None),
        P(DP, None),
        P(DP),
        P(None, MP),
        P(MP, None),
        P(DP + MP, None),
        P(DP + MP),
    )
    return jax.shard_map(
        body,
        mesh=split,
        in_specs=placed,
        out_specs=(P(None, MP), P(MP, None), P(DP + MP, None), P(DP + MP)),
        check_vma=False,
    )
```

time: 118 us -> 117 us (level); the launches traced: 118 us -> 115 us
  Pallas kernels: 0 us -> 6.9 us
  matrix products: 5.88 us -> 0.9 us
  local copies, waits for them, and re-layouts: 9.08 us -> 4.9 us
    pallas_call x0 -> x3, Pallas kernels: none -> 6.9 us  [with_vmem(): run(*(pltpu.with_memory_space_constraint(t, pltpu.HBM if i in loose else...]
    dot_general x13 -> x2, matrix products: 5.88 us -> 0.9 us  [the longest x1 0.61 us: body(): lax.dot_general(layer_input, dpre, (((0,), (0,)), ((), ())), precision=la...]
    unnamed x17 -> x13, local copies, waits for them, and re-layouts: 5.01 us -> 2.79 us
    dot_general x2 -> x0, local copies, waits for them, and re-layouts: 1.19 us -> none  [dot(): lax.dot_general(left, right, ((dims[:1], dims[1:]), ((), ())), precision=...]
    all_gather x1 -> x2, blocking collectives: 14.9 us -> 14.8 us  [the longest x1 9.54 us: body(): lax.all_gather(lax.all_gather(mine, 'c', tiled=False), 'y', tiled=False)]
where the time goes in v4:
time: 117 us; the launch traced here: 115 us
  blocking collectives  66.3 us (57%)
  starting transfers between devices  19.3 us (16%)
  waiting for transfers between devices  12.3 us (11%)
  Pallas kernels  6.9 us (6%)
  local copies, waits for them, and re-layouts  4.9 us (4%)
  between operations  3.28 us (3%)
  other arithmetic  1.28 us (1%)
    all_to_all x1, blocking collectives, body(): buf = jnp.sum(lax.all_to_all(buf, 'h', 0, 0, tiled=True), axis=0)  26.2 us
    all_to_all x1, blocking collectives, body(): buf = jnp.sum(lax.all_to_all(buf, XL, 0, 0, tiled=True), axis=0)  25.4 us
    all_to_all x1, starting transfers between devices, body(): stats = lax.all_to_all(stats, MP, 0, 0, tiled=True)  10.2 us
    all_gather x1, blocking collectives, body(): lax.all_gather(lax.all_gather(mine, 'c', tiled=False), 'y', tiled=False)  9.54 us
    all_to_all x1, waiting for transfers between devices, body(): part = lax.all_to_all(part.reshape(n_mp, fblk, count), MP, 0, 0, tiled=True)  7.72 us
    pallas_call x3, Pallas kernels, with_vmem(): run(*(pltpu.with_memory_space_constraint(t, pltpu.HBM if i in loose else...  6.9 us
    all_gather x1, blocking collectives, body(): lax.all_gather(mine, 'c', tiled=False)  5.27 us
    all_to_all x1, starting transfers between devices, body(): full = lax.all_to_all(full, XL, 0, 0, tiled=True)  4.93 us
  transfers between devices with their start and end apart: 3, of which 2 were waited for; matrix products, arithmetic and copies ran while one was open for 2% of the time, Pallas kernels for 0%

profile of v4, /device:TPU:1, one launch (start us, length us, event | category | flops | bytes accessed | tf_op | source)
XLA Modules:
  0.0 115.1 jit_solution(10276478688396507392)
XLA Ops:
  0.6 3.9 %shard_map.111 = (f32[256,256]{1,0:T(8,128)S(1)}, f32[256,256]{1,0:T(8,128)S(1)}, f32[256,256]{1,0:T(8,128)S(1)}, f32[256,256]{1,0:T(8,128)S(1)}, f32[256,128]{1,0:T(8,128)S(1)}, /*index=5*/f32[8,8,128]{2,1,0:T(8,128)}) custom-call(f32[256,512]{1,0:T(8,128)} %refs_0_.1, f32[512,256]{1,0:T(8,128)} %w_ref.1, f32[256,512]{1,0:T(8,128)} %refs_2_.1, ...), custom_call_target="tpu_custom_call" | custom-call | tf_op jit(solution)/shard_map/pallas_call | solution.py:156
  4.6 10.2 %all-to-all-start = ((f32[8,8,128]{2,1,0:T(8,128)}), f32[8,8,128]{2,1,0:T(8,128)S(1)}, u32[]{:S(2)}, u32[]{:S(2)}) async-start(f32[8,8,128]{2,1,0:T(8,128)} %get-tuple-element.13), calls=%async_computation | async-start | bytes 65536 | tf_op jit(solution)/shard_map/all_to_all | solution.py:178
  14.8 0.1 constant_dynamic-slice_fusion
  15.0 4.5 %all-to-all-done.st_ref = f32[8,8,128]{2,1,0:T(8,128)S(1)} async-done(((f32[8,8,128]{2,1,0:T(8,128)}), f32[8,8,128]{2,1,0:T(8,128)S(1)}, u32[]{:S(2)}, u32[]{:S(2)}) %all-to-all-start) | async-done | bytes 32800 | tf_op jit(solution)/shard_map/all_to_all | solution.py:178
  19.5 2.6 %shard_map.112 = (f32[256,256]{1,0:T(8,128)S(1)}, f32[256,64]{1,0:T(8,128)S(1)}, f32[512,256]{1,0:T(8,128)}) custom-call(f32[8,8,128]{2,1,0:T(8,128)S(1)} %all-to-all-done.st_ref, f32[256,256]{1,0:T(8,128)S(1)} %get-tuple-element.14.act_ref, f32[256,256]{1,0:T(8,128)S(1)} %get-tuple-element.15.dfac_ref, f32[256,256]{1,0:T(8,128)S(1)} %get-tuple-element.16.attn_ref, ...), custom_call_target="tpu_custom_call" | custom-call | tf_op jit(solution)/shard_map/pallas_call | solution.py:156
  22.1 4.1 %all-to-all-start.1 = ((f32[8,64,256]{2,1,0:T(8,128)}), f32[8,64,256]{2,1,0:T(8,128)S(1)}, u32[]{:S(2)}, u32[]{:S(2)}) async-start(f32[8,64,256]{2,1,0:T(8,128)} %bitcast), calls=%async_computation.1 | async-start | bytes 1048576 | tf_op jit(solution)/shard_map/all_to_all | solution.py:182
  26.3 0.3 fusion.w2_ref
  26.6 0.7 copy-done.3
  27.3 0.6 convolution_bitcast_fusion.w1_ref
  27.9 7.7 %all-to-all-done.1.recv_ref = f32[8,64,256]{2,1,0:T(8,128)S(1)} async-done(((f32[8,64,256]{2,1,0:T(8,128)}), f32[8,64,256]{2,1,0:T(8,128)S(1)}, u32[]{:S(2)}, u32[]{:S(2)}) %all-to-all-start.1) | async-done | bytes 524320 | tf_op jit(solution)/shard_map/all_to_all | solution.py:182
  35.6 0.7 copy-done.1
  36.3 0.4 shard_map.113
  36.7 25.4 %all_to_all.25 = f32[16,96,128]{2,1,0:T(8,128)S(1)} all-to-all(f32[16,96,128]{2,1,0:T(8,128)S(1)} %shard_map.113), channel_id=1, replica_groups=mesh['x'=4,'h'=4,'l'=4,'y'=4,'c'=2] {'x','l'}, dimensions={0} | all-to-all | bytes 1572864 | tf_op jit(solution)/shard_map/all_to_all | solution.py:190
  62.1 26.2 %all_to_all.26 = f32[4,96,128]{2,1,0:T(8,128)S(1)} all-to-all(f32[4,96,128]{2,1,0:T(8,128)S(1)} %broadcast_in_dim.4), channel_id=1, replica_groups=mesh['x'=4,'h'=4,'l'=4,'y'=4,'c'=2] {'h'}, dimensions={0} | all-to-all | bytes 393216 | tf_op jit(solution)/shard_map/all_to_all | solution.py:192
  88.3 0.9 broadcast_in_dim.5
  89.2 4.9 %all-to-all-start.4 = ((f32[16,80,128]{2,1,0:T(8,128)}), f32[16,80,128]{2,1,0:T(8,128)S(1)}, u32[]{:S(2)}, u32[]{:S(2)}) async-start(f32[16,80,128]{2,1,0:T(8,128)} %broadcast_in_dim.5), calls=%async_computation.4 | async-start | bytes 1310720 | tf_op jit(solution)/shard_map/all_to_all | solution.py:194
  94.9 5.3 %all-gather.2 = f32[2,4,128]{2,1,0:T(4,128)S(1)} all-gather(f32[1,4,128]{2,1,0:T(4,128)S(1)} %dynamic-slice_bitcast_fusion), channel_id=2, replica_groups=mesh['x'=4,'h'=4,'l'=4,'y'=4,'c'=2] {'c'}, dimensions={0}, use_global_device_ids=true | all-gather | bytes 6144 | tf_op jit(solution)/shard_map/all_gather | solution.py:198
  100.1 9.5 %all-gather.1 = f32[8,4,128]{2,1,0:T(4,128)S(1)} all-gather(f32[2,4,128]{2,1,0:T(4,128)S(1)} %all-gather.2), channel_id=3, replica_groups=mesh['x'=4,'h'=4,'l'=4,'y'=4,'c'=2] {'y'}, dimensions={0}, use_global_device_ids=true | all-gather | bytes 20480 | tf_op jit(solution)/shard_map/all_gather | solution.py:198
  109.7 0.1 reshape.63
  109.8 0.6 multiply_reduce_fusion.1
  111.2 0.6 copy-done.4
  111.8 0.6 sub.8
  112.5 0.7 copy.31
  113.2 0.8 slice.13
  (19 shorter events, 0.4 us)
Async XLA Ops:
  0.6 14.2 %copy-start.2 = (f32[256,512]{1,0:T(8,128)S(1)}, f32[256,512]{1,0:T(8,128)}, u32[]{:S(2)}) copy-start(f32[256,512]{1,0:T(8,128)} %refs_2_.1) | copy-start | bytes 1572868
  4.6 15.0 %copy-start = (f32[512,256]{1,0:T(8,128)S(1)}, f32[512,256]{1,0:T(8,128)}, u32[]{:S(2)}) copy-start(f32[512,256]{1,0:T(8,128)} %w_ref.1) | copy-start | bytes 1572868
  4.6 15.0 %all-to-all-start = ((f32[8,8,128]{2,1,0:T(8,128)}), f32[8,8,128]{2,1,0:T(8,128)S(1)}, u32[]{:S(2)}, u32[]{:S(2)}) async-start(f32[8,8,128]{2,1,0:T(8,128)} %get-tuple-element.13), calls=%async_computation | async-start | bytes 65536 | tf_op jit(solution)/shard_map/all_to_all | solution.py:178
  22.1 13.5 %all-to-all-start.1 = ((f32[8,64,256]{2,1,0:T(8,128)}), f32[8,64,256]{2,1,0:T(8,128)S(1)}, u32[]{:S(2)}, u32[]{:S(2)}) async-start(f32[8,64,256]{2,1,0:T(8,128)} %bitcast), calls=%async_computation.1 | async-start | bytes 1048576 | tf_op jit(solution)/shard_map/all_to_all | solution.py:182
  26.3 1.0 copy-start.3
  35.6 0.7 copy-start.1
  89.2 23.2 %all-to-all-start.4 = ((f32[16,80,128]{2,1,0:T(8,128)}), f32[16,80,128]{2,1,0:T(8,128)S(1)}, u32[]{:S(2)}, u32[]{:S(2)}) async-start(f32[16,80,128]{2,1,0:T(8,128)} %broadcast_in_dim.5), calls=%async_computation.4 | async-start | bytes 1310720 | tf_op jit(solution)/shard_map/all_to_all | solution.py:194
  111.1 0.7 copy-start.4

commit v5 on v4

--- a/solution.py
+++ b/solution.py
@@ -195,7 +195,7 @@
     w1g = full[:, :64].reshape(n_xl, 4, 2, 8, 128).transpose(0, 1, 3, 2, 4).reshape(width, 4 * hd)
     w2g = full[:, 64:].reshape(n_x, n_l, 16, 128).transpose(1, 2, 0, 3).reshape(hd, width)
     mine = lax.dynamic_slice(buf, (80 + half * lax.axis_index("h"), 0), (half, 128))
-    mine = lax.all_gather(lax.all_gather(mine, "c", tiled=False), "y", tiled=False)
+    mine = lax.all_gather(mine, MP, tiled=False)
     mine = mine.reshape(n_mp, half, 2, fblk)
     who = lax.axis_index(MP)
     row_grad = lax.dynamic_slice(mine, (0, who % half, who // half, 0), (n_mp, 1, 1, fblk)).reshape(1, width)

time: 117 us -> 116 us (level)
    all_gather x2 -> x1, blocking collectives: 14.8 us -> 14.9 us  [body(): mine = lax.all_gather(mine, MP, tiled=False)]
where the time goes in v5:
time: 116 us; the launch traced here: 115 us
  blocking collectives  66.4 us (57%)
  starting transfers between devices  19.3 us (17%)
  waiting for transfers between devices  12.3 us (11%)
  Pallas kernels  6.9 us (6%)
  local copies, waits for them, and re-layouts  4.9 us (4%)
  between operations  3.28 us (3%)
  other arithmetic  1.28 us (1%)
    all_to_all x1, blocking collectives, body(): buf = jnp.sum(lax.all_to_all(buf, 'h', 0, 0, tiled=True), axis=0)  26.2 us
    all_to_all x1, blocking collectives, body(): buf = jnp.sum(lax.all_to_all(buf, XL, 0, 0, tiled=True), axis=0)  25.4 us
    all_gather x1, blocking collectives, body(): mine = lax.all_gather(mine, MP, tiled=False)  14.9 us
    all_to_all x1, starting transfers between devices, body(): stats = lax.all_to_all(stats, MP, 0, 0, tiled=True)  10.2 us
    all_to_all x1, waiting for transfers between devices, body(): part = lax.all_to_all(part.reshape(n_mp, fblk, count), MP, 0, 0, tiled=True)  7.72 us
    pallas_call x3, Pallas kernels, with_vmem(): run(*(pltpu.with_memory_space_constraint(t, pltpu.HBM if i in loose else...  6.9 us
    all_to_all x1, starting transfers between devices, body(): full = lax.all_to_all(full, XL, 0, 0, tiled=True)  4.93 us
    all_to_all x1, waiting for transfers between devices, body(): stats = lax.all_to_all(stats, MP, 0, 0, tiled=True)  4.54 us
  transfers between devices with their start and end apart: 3, of which 2 were waited for; matrix products, arithmetic and copies ran while one was open for 2% of the time, Pallas kernels for 0%

profile of v5, /device:TPU:1, one launch (start us, length us, event | category | flops | bytes accessed | tf_op | source)
XLA Modules:
  0.0 115.2 jit_solution(3168475194103874517)
XLA Ops:
  0.6 3.9 %shard_map.111 = (f32[256,256]{1,0:T(8,128)S(1)}, f32[256,256]{1,0:T(8,128)S(1)}, f32[256,256]{1,0:T(8,128)S(1)}, f32[256,256]{1,0:T(8,128)S(1)}, f32[256,128]{1,0:T(8,128)S(1)}, /*index=5*/f32[8,8,128]{2,1,0:T(8,128)}) custom-call(f32[256,512]{1,0:T(8,128)} %refs_0_.1, f32[512,256]{1,0:T(8,128)} %w_ref.1, f32[256,512]{1,0:T(8,128)} %refs_2_.1, ...), custom_call_target="tpu_custom_call" | custom-call | tf_op jit(solution)/shard_map/pallas_call | solution.py:156
  4.6 10.2 %all-to-all-start = ((f32[8,8,128]{2,1,0:T(8,128)}), f32[8,8,128]{2,1,0:T(8,128)S(1)}, u32[]{:S(2)}, u32[]{:S(2)}) async-start(f32[8,8,128]{2,1,0:T(8,128)} %get-tuple-element.13), calls=%async_computation | async-start | bytes 65536 | tf_op jit(solution)/shard_map/all_to_all | solution.py:178
  14.8 0.1 constant_dynamic-slice_fusion
  15.0 4.5 %all-to-all-done.st_ref = f32[8,8,128]{2,1,0:T(8,128)S(1)} async-done(((f32[8,8,128]{2,1,0:T(8,128)}), f32[8,8,128]{2,1,0:T(8,128)S(1)}, u32[]{:S(2)}, u32[]{:S(2)}) %all-to-all-start) | async-done | bytes 32800 | tf_op jit(solution)/shard_map/all_to_all | solution.py:178
  19.5 2.6 %shard_map.112 = (f32[256,256]{1,0:T(8,128)S(1)}, f32[256,64]{1,0:T(8,128)S(1)}, f32[512,256]{1,0:T(8,128)}) custom-call(f32[8,8,128]{2,1,0:T(8,128)S(1)} %all-to-all-done.st_ref, f32[256,256]{1,0:T(8,128)S(1)} %get-tuple-element.14.act_ref, f32[256,256]{1,0:T(8,128)S(1)} %get-tuple-element.15.dfac_ref, f32[256,256]{1,0:T(8,128)S(1)} %get-tuple-element.16.attn_ref, ...), custom_call_target="tpu_custom_call" | custom-call | tf_op jit(solution)/shard_map/pallas_call | solution.py:156
  22.1 4.1 %all-to-all-start.1 = ((f32[8,64,256]{2,1,0:T(8,128)}), f32[8,64,256]{2,1,0:T(8,128)S(1)}, u32[]{:S(2)}, u32[]{:S(2)}) async-start(f32[8,64,256]{2,1,0:T(8,128)} %bitcast), calls=%async_computation.1 | async-start | bytes 1048576 | tf_op jit(solution)/shard_map/all_to_all | solution.py:182
  26.3 0.3 fusion.w2_ref
  26.6 0.7 copy-done.3
  27.3 0.6 convolution_bitcast_fusion.w1_ref
  27.9 7.7 %all-to-all-done.1.recv_ref = f32[8,64,256]{2,1,0:T(8,128)S(1)} async-done(((f32[8,64,256]{2,1,0:T(8,128)}), f32[8,64,256]{2,1,0:T(8,128)S(1)}, u32[]{:S(2)}, u32[]{:S(2)}) %all-to-all-start.1) | async-done | bytes 524320 | tf_op jit(solution)/shard_map/all_to_all | solution.py:182
  35.6 0.7 copy-done.1
  36.3 0.4 shard_map.113
  36.7 25.4 %all_to_all.25 = f32[16,96,128]{2,1,0:T(8,128)S(1)} all-to-all(f32[16,96,128]{2,1,0:T(8,128)S(1)} %shard_map.113), channel_id=1, replica_groups=mesh['x'=4,'h'=4,'l'=4,'y'=4,'c'=2] {'x','l'}, dimensions={0} | all-to-all | bytes 1572864 | tf_op jit(solution)/shard_map/all_to_all | solution.py:190
  62.1 26.2 %all_to_all.26 = f32[4,96,128]{2,1,0:T(8,128)S(1)} all-to-all(f32[4,96,128]{2,1,0:T(8,128)S(1)} %broadcast_in_dim.4), channel_id=1, replica_groups=mesh['x'=4,'h'=4,'l'=4,'y'=4,'c'=2] {'h'}, dimensions={0} | all-to-all | bytes 393216 | tf_op jit(solution)/shard_map/all_to_all | solution.py:192
  88.3 0.9 broadcast_in_dim.5
  89.2 4.9 %all-to-all-start.4 = ((f32[16,80,128]{2,1,0:T(8,128)}), f32[16,80,128]{2,1,0:T(8,128)S(1)}, u32[]{:S(2)}, u32[]{:S(2)}) async-start(f32[16,80,128]{2,1,0:T(8,128)} %broadcast_in_dim.5), calls=%async_computation.4 | async-start | bytes 1310720 | tf_op jit(solution)/shard_map/all_to_all | solution.py:194
  94.9 14.9 %all-gather.1 = f32[8,4,128]{2,1,0:T(4,128)S(1)} all-gather(f32[1,4,128]{2,1,0:T(4,128)S(1)} %dynamic-slice_bitcast_fusion), channel_id=2, replica_groups=mesh['x'=4,'h'=4,'l'=4,'y'=4,'c'=2] {'y','c'}, dimensions={0}, use_global_device_ids=true | all-gather | bytes 18432 | tf_op jit(solution)/shard_map/all_gather | solution.py:198
  109.8 0.1 reshape.63
  109.9 0.6 multiply_reduce_fusion.1
  111.3 0.6 copy-done.4
  111.9 0.6 sub.8
  112.5 0.1 copy.25
  112.6 0.7 copy.31
  113.3 0.8 slice.13
  (18 shorter events, 0.3 us)
Async XLA Ops:
  0.6 14.2 %copy-start.2 = (f32[256,512]{1,0:T(8,128)S(1)}, f32[256,512]{1,0:T(8,128)}, u32[]{:S(2)}) copy-start(f32[256,512]{1,0:T(8,128)} %refs_2_.1) | copy-start | bytes 1572868
  4.6 15.0 %copy-start = (f32[512,256]{1,0:T(8,128)S(1)}, f32[512,256]{1,0:T(8,128)}, u32[]{:S(2)}) copy-start(f32[512,256]{1,0:T(8,128)} %w_ref.1) | copy-start | bytes 1572868
  4.6 15.0 %all-to-all-start = ((f32[8,8,128]{2,1,0:T(8,128)}), f32[8,8,128]{2,1,0:T(8,128)S(1)}, u32[]{:S(2)}, u32[]{:S(2)}) async-start(f32[8,8,128]{2,1,0:T(8,128)} %get-tuple-element.13), calls=%async_computation | async-start | bytes 65536 | tf_op jit(solution)/shard_map/all_to_all | solution.py:178
  22.1 13.5 %all-to-all-start.1 = ((f32[8,64,256]{2,1,0:T(8,128)}), f32[8,64,256]{2,1,0:T(8,128)S(1)}, u32[]{:S(2)}, u32[]{:S(2)}) async-start(f32[8,64,256]{2,1,0:T(8,128)} %bitcast), calls=%async_computation.1 | async-start | bytes 1048576 | tf_op jit(solution)/shard_map/all_to_all | solution.py:182
  26.3 1.0 copy-start.3
  35.6 0.7 copy-start.1
  89.2 23.3 %all-to-all-start.4 = ((f32[16,80,128]{2,1,0:T(8,128)}), f32[16,80,128]{2,1,0:T(8,128)S(1)}, u32[]{:S(2)}, u32[]{:S(2)}) async-start(f32[16,80,128]{2,1,0:T(8,128)} %broadcast_in_dim.5), calls=%async_computation.4 | async-start | bytes 1310720 | tf_op jit(solution)/shard_map/all_to_all | solution.py:194
  111.2 0.7 copy-start.4
